TPU v7x, 32 devices: a whole 2x2x4 slice. The times are simulated.
32 devices in a mesh: seq: 8 (over z, x), doc: 4 (over y, core).
Axes of the slice: x: 2, y: 2, z: 4, core: 2. Of those that a mesh axis runs over, the one named last changes fastest.
Arguments:
- tokens: bfloat16 [16, 8192, 512], P('doc', 'seq'), may hold values from -6 to 6
- factor_one: bfloat16 [8, 1024, 1024], P('seq'), may hold values from -0.1875 to 0.1875
- factor_two: bfloat16 [1024, 8, 8], P('seq'), may hold values from -2 to 2
- gate_gain: float32 [512], replicated, may hold values from 0.5 to 2
- gate_bias: float32 [512], replicated, may hold values from -4 to 4
- block_counts: int32 [16], replicated, may hold values from 7 to 8, as said below
- partner: int32 [16], replicated, may hold values from 0 to 15, as said below
- reading: float32 [512, 256], replicated, may hold values from -0.25 to 0.25
Outputs:
- gated: bfloat16 [16, 8, 1024, 512], P('doc', None, 'seq')
- contrast: float32 [16, 256], P('doc')
Inputs may be any that keep to these rules, and one draw needn't show every extreme that they name: `block_counts`: some document has all 8 blocks valid and another exactly 7. partner is a single cycle through all documents; no document is its own partner.
All inputs are finite; a program needn't handle non-finite values.
Results may differ from a plain program's by a relative error of at most 0.005.
Values may be sent and summed in bfloat16 or wider, within the bound.
A program may use at most 128 MiB of HBM per device.

v0:
```python
import jax
import jax.numpy as jnp
from jax import lax
from jax.sharding import PartitionSpec as P


def shards(tokens, factor_one, factor_two, gate_gain, gate_bias, block_counts, partner, reading):
    doc_dev, tok_dev, chan = tokens.shape
    blocks_dev, blk_size = (factor_one.shape[0], factor_one.shape[1])
    all_blocks = factor_two.shape[1]
    all_docs = block_counts.shape[0]
    doc_start = lax.axis_index("doc") * doc_dev
    block_start = lax.axis_index("seq") * blocks_dev
    local_counts = lax.dynamic_slice_in_dim(block_counts, doc_start, doc_dev)
    block_ids = block_start + jnp.arange(blocks_dev, dtype=jnp.int32)
    inside = (block_ids[None, :] < local_counts[:, None]).astype(jnp.bfloat16)
    grid = tokens.reshape(doc_dev, blocks_dev, blk_size, chan) * inside[:, :, None, None]
    mixed = jnp.einsum(
        "dbic,bij->dbjc", grid, factor_one, preferred_element_type=jnp.float32
    ).astype(jnp.bfloat16)
    values_t, inputs_t = (
        lax.all_to_all(mixed, "seq", split_axis=2, concat_axis=1, tiled=True),
        lax.all_to_all(grid, "seq", split_axis=2, concat_axis=1, tiled=True),
    )
    second = jnp.einsum("dpjc,jpq->dqjc", values_t, factor_two, preferred_element_type=jnp.float32)
    gate = jax.nn.sigmoid(gate_gain * inputs_t.astype(jnp.float32) + gate_bias)
    full = second * gate
    gated = full.astype(jnp.bfloat16)
    row_ids = jnp.arange(all_blocks, dtype=jnp.int32)
    keep = (row_ids[None, :] < local_counts[:, None]).astype(jnp.float32)
    partial_value = jnp.sum(full * keep[:, :, None, None], axis=(1, 2))
    scale_local = 1.0 / jnp.sqrt(local_counts.astype(jnp.float32) * blk_size)
    mine = lax.psum(partial_value, "seq") * scale_local[:, None]
    pooled_all = lax.all_gather(mine, "doc", axis=0, tiled=True)
    local_partner = lax.dynamic_slice_in_dim(partner, doc_start, doc_dev)
    picker = (local_partner[:, None] == jnp.arange(all_docs, dtype=jnp.int32)[None, :]).astype(
        jnp.float32
    )
    other = jnp.dot(picker, pooled_all, precision=lax.Precision.HIGHEST)
    contrast = jnp.dot(mine - other, reading, precision=lax.Precision.HIGHEST)
    return (gated, contrast)


def solution(mesh):
    placed = (
        P("doc", "seq", None),
        P("seq", None, None),
        P("seq", None, None),
        P(),
        P(),
        P(),
        P(),
        P(),
    )
    return jax.shard_map(
        shards,
        mesh=mesh,
        in_specs=placed,
        out_specs=(P("doc", None, "seq", None), P("doc", None)),
        check_vma=False,
    )
```

profile of v0, /device:TPU:0, one launch (start us, length us, event | category | flops | bytes accessed | tf_op | source)
XLA Modules:
  0.0 254.0 jit_solution(281498161123050045)
XLA Ops:
  0.6 0.0 copy-start
  0.7 0.9 multiply_rsqrt_fusion
  1.5 7.5 %fusion.21 = bf16[4,1,1024,512]{3,0,1,2:T(4,128)(2,1)} fusion(bf16[4]{0:T(256)(128)(2,1)S(1)} %compare_convert_fusion, bf16[4,1024,512]{2,1,0:T(8,128)(2,1)} %param.8), kind=kLoop, calls=%fused_computation.24 | loop fusion | flops 2097152 | bytes 8388616 | tf_op jit(solution)/shard_map/mul | solution.py:17
  9.0 7.3 %all-to-all-start.1 = ((bf16[4,1,1024,512]{3,0,1,2:T(4,128)(2,1)}), bf16[4,1,1024,512]{3,0,1,2:T(4,128)(2,1)}, u32[]{:S(2)}, u32[]{:S(2)}) async-start(bf16[4,1,1024,512]{3,0,1,2:T(4,128)(2,1)} %fusion.21), calls=%async_computation.1 | async-start | bytes 8388608 | tf_op jit(solution)/shard_map/all_to_all | solution.py:23
  16.2 5.4 %copy_multiply_fusion.1 = bf16[4,1024,512]{2,0,1:T(4,128)(2,1)S(1)} fusion(bf16[4,1024,512]{2,1,0:T(8,128)(2,1)} %param.8, bf16[4]{0:T(256)(128)(2,1)S(1)} %compare_convert_fusion), kind=kLoop, calls=%fused_computation.12 | loop fusion | flops 2097152 | bytes 8388616 | tf_op jit(solution)/shard_map/mul | solution.py:17
  21.7 0.0 copy-done
  21.7 6.5 %convert_bitcast_fusion = bf16[4,1,1024,512]{2,3,0,1:T(8,128)(2,1)} fusion(bf16[4,1024,512]{2,0,1:T(4,128)(2,1)S(1)} %copy_multiply_fusion.1, bf16[1,1024,1024]{2,1,0:T(8,128)(2,1)S(1)} %copy-done), kind=kOutput, calls=%fused_computation.13 | convolution fusion | flops 4297064448 | bytes 10485760 | tf_op jit(solution)/shard_map/dbic,bij->dbjc/dot_general | solution.py:18
  28.2 7.9 %copy.28 = bf16[4,1,1024,512]{3,0,1,2:T(4,128)(2,1)} copy(bf16[4,1,1024,512]{2,3,0,1:T(8,128)(2,1)} %convert_bitcast_fusion) | data formatting | bytes 8388608 | tf_op jit(solution)/shard_map/convert_element_type | solution.py:20
  36.0 0.0 copy-start.5
  36.0 0.0 copy-start.2
  36.0 73.5 %all-to-all-done.1 = bf16[4,1,1024,512]{3,0,1,2:T(4,128)(2,1)} async-done(((bf16[4,1,1024,512]{3,0,1,2:T(4,128)(2,1)}), bf16[4,1,1024,512]{3,0,1,2:T(4,128)(2,1)}, u32[]{:S(2)}, u32[]{:S(2)}) %all-to-all-start.1) | async-done | bytes 4194336 | tf_op jit(solution)/shard_map/all_to_all | solution.py:23
  109.5 4.8 %all-to-all-start = ((bf16[4,1,1024,512]{3,0,1,2:T(4,128)(2,1)}), bf16[4,1,1024,512]{3,0,1,2:T(4,128)(2,1)}, u32[]{:S(2)}, u32[]{:S(2)}) async-start(bf16[4,1,1024,512]{3,0,1,2:T(4,128)(2,1)} %copy.28), calls=%async_computation | async-start | bytes 8388608 | tf_op jit(solution)/shard_map/all_to_all | solution.py:22
  114.3 0.0 copy-done.5
  114.3 0.1 dynamic_slice.7
  114.4 0.0 copy-done.2
  114.4 0.2 copy.35
  114.6 0.1 fusion.14
  114.7 3.0 %copy.32 = bf16[4,1,1024,512]{3,2,0,1:T(8,128)(2,1)S(1)} copy(bf16[4,1,1024,512]{3,0,1,2:T(4,128)(2,1)} %all-to-all-done.1) | data formatting | bytes 8388608 | tf_op jit(solution)/shard_map/all_to_all | solution.py:23
  117.7 0.0 copy-start.3
  117.7 0.0 copy-start.4
  117.7 4.4 %convert.1 = f32[4,8,128,512]{3,2,1,0:T(8,128)} convert(bf16[4,8,128,512]{3,2,1,0:T(8,128)(2,1)S(1)} %bitcast.24) | non-fusion elementwise | flops 2097152 | bytes 12582912 | tf_op jit(solution)/shard_map/convert_element_type | solution.py:26
  122.1 84.6 %all-to-all-done = bf16[4,1,1024,512]{3,0,1,2:T(4,128)(2,1)} async-done(((bf16[4,1,1024,512]{3,0,1,2:T(4,128)(2,1)}), bf16[4,1,1024,512]{3,0,1,2:T(4,128)(2,1)}, u32[]{:S(2)}, u32[]{:S(2)}) %all-to-all-start) | async-done | bytes 4194336 | tf_op jit(solution)/shard_map/all_to_all | solution.py:22
  206.7 0.0 copy-done.3
  206.7 0.0 copy-done.4
  206.7 14.7 %multiply_reduce_fusion = (f32[4,512]{1,0:T(4,128)S(1)}, bf16[4,8,128,512]{3,1,0,2:T(8,128)(2,1)}) fusion(f32[4,8]{1,0:T(4,128)S(1)} %fusion.14, f32[512]{0:T(512)S(1)} %copy-done.3, f32[4,8,128,512]{3,2,1,0:T(8,128)} %convert.1, f32[512]{0:T(512)S(1)} %copy-done.4, bf16[128,8,8,1]{1,2,3,0:T(8,128)(2,1)S(1)} %copy.35, bf16[4,8,128,512]{3,0,2,1:T(4,128)(2,1)} %bitcast.5), kind=kOutput, calls=%fused_computation.7 | convolution fusion | flops 52426752 | bytes 16806016 | tf_op jit(solution)/shard_map/dpjc,jpq->dqjc/dot_general | solution.py:25
  221.4 19.6 %psum.7 = f32[4,512]{1,0:T(4,128)S(1)} all-reduce(f32[4,512]{1,0:T(4,128)S(1)} %get-tuple-element.12), channel_id=1, replica_groups=mesh['seq'=8,'doc'=4] {'seq'}, use_global_device_ids=true, to_apply=%region_1.0 | all-reduce | flops 2048 | bytes 16384 | tf_op jit(solution)/shard_map/psum | solution.py:33
  241.0 0.1 multiply_bitcast_fusion
  241.1 5.2 %all-gather = f32[4,4,512]{2,1,0:T(4,128)S(1)} all-gather(f32[1,4,512]{2,1,0:T(4,128)S(1)} %multiply_bitcast_fusion), channel_id=1, replica_groups=mesh['seq'=8,'doc'=4] {'doc'}, dimensions={0}, use_global_device_ids=true | all-gather | bytes 40960 | tf_op jit(solution)/shard_map/all_gather | solution.py:34
  246.3 0.0 copy-start.1
  246.3 6.6 %copy.34 = bf16[4,8,128,512]{3,2,1,0:T(8,128)(2,1)} copy(bf16[4,8,128,512]{3,1,0,2:T(8,128)(2,1)} %get-tuple-element.13) | data formatting | bytes 8388608
  252.9 0.2 convolution_subtract_fusion
  253.1 0.0 copy-done.1
  253.1 0.9 fusion.16
  (2 shorter events, 0.0 us)
Async XLA Ops:
  0.6 21.1 %copy-start = (bf16[1,1024,1024]{2,1,0:T(8,128)(2,1)S(1)}, bf16[1,1024,1024]{2,1,0:T(8,128)(2,1)}, u32[]{:S(2)}) copy-start(bf16[1,1024,1024]{2,1,0:T(8,128)(2,1)} %param.9) | copy-start | bytes 6291460
  9.0 100.5 %all-to-all-start.1 = ((bf16[4,1,1024,512]{3,0,1,2:T(4,128)(2,1)}), bf16[4,1,1024,512]{3,0,1,2:T(4,128)(2,1)}, u32[]{:S(2)}, u32[]{:S(2)}) async-start(bf16[4,1,1024,512]{3,0,1,2:T(4,128)(2,1)} %fusion.21), calls=%async_computation.1 | async-start | bytes 8388608 | tf_op jit(solution)/shard_map/all_to_all | solution.py:23
  36.0 78.3 %copy-start.5 = (s32[16]{0:T(128)S(1)}, s32[16]{0:T(128)}, u32[]{:S(2)}) copy-start(s32[16]{0:T(128)} %param.14) | copy-start | bytes 196
  36.0 78.4 %copy-start.2 = (bf16[128,8,8]{0,2,1:T(8,128)(2,1)S(1)}, bf16[128,8,8]{0,2,1:T(8,128)(2,1)}, u32[]{:S(2)}) copy-start(bf16[128,8,8]{0,2,1:T(8,128)(2,1)} %param.10) | copy-start | bytes 49156
  109.5 97.2 %all-to-all-start = ((bf16[4,1,1024,512]{3,0,1,2:T(4,128)(2,1)}), bf16[4,1,1024,512]{3,0,1,2:T(4,128)(2,1)}, u32[]{:S(2)}, u32[]{:S(2)}) async-start(bf16[4,1,1024,512]{3,0,1,2:T(4,128)(2,1)} %copy.28), calls=%async_computation | async-start | bytes 8388608 | tf_op jit(solution)/shard_map/all_to_all | solution.py:22
  117.7 89.0 %copy-start.3 = (f32[512]{0:T(512)S(1)}, f32[512]{0:T(512)}, u32[]{:S(2)}) copy-start(f32[512]{0:T(512)} %param.12) | copy-start | bytes 6148
  117.7 89.0 %copy-start.4 = (f32[512]{0:T(512)S(1)}, f32[512]{0:T(512)}, u32[]{:S(2)}) copy-start(f32[512]{0:T(512)} %param.11) | copy-start | bytes 6148
  246.3 6.8 %copy-start.1 = (f32[512,256]{1,0:T(8,128)S(1)}, f32[512,256]{1,0:T(8,128)}, u32[]{:S(2)}) copy-start(f32[512,256]{1,0:T(8,128)} %param.15) | copy-start | bytes 1572868
where the time goes:
time: 255 us; the launch traced here: 254 us
  waiting for transfers between devices  158 us (62%)
  blocking collectives  24.8 us (10%)
  matrix products  22.2 us (9%)
  other arithmetic  18.3 us (7%)
  local copies, waits for them, and re-layouts  17.8 us (7%)
  starting transfers between devices  12 us (5%)
    all_to_all x1, waiting for transfers between devices, shards(): lax.all_to_all(mixed, 'seq', split_axis=2, concat_axis=1, tiled=True)  84.6 us
    all_to_all x1, waiting for transfers between devices, shards(): lax.all_to_all(grid, 'seq', split_axis=2, concat_axis=1, tiled=True)  73.5 us
    psum x1, blocking collectives, shards(): mine = lax.psum(partial_value, 'seq') * scale_local[:, None]  19.6 us
    dot_general x1, matrix products, shards(): jnp.einsum('dpjc,jpq->dqjc', values_t, factor_two, preferred_element_type...  14.7 us
    mul x2, other arithmetic, shards(): tokens.reshape(doc_dev, blocks_dev, blk_size, chan)  12.9 us
    convert_element_type x1, local copies, waits for them, and re-layouts, shards(): mixed = jnp.einsum('dbic,bij->dbjc', grid, factor_one, preferred_element_...  7.88 us
    all_to_all x1, starting transfers between devices, shards(): lax.all_to_all(grid, 'seq', split_axis=2, concat_axis=1, tiled=True)  7.25 us
    unnamed x15, local copies, waits for them, and re-layouts  6.85 us
  transfers between devices with their start and end apart: 2, of which 2 were waited for; matrix products, arithmetic and copies ran while one was open for 11% of the time, Pallas kernels for 0%

commit v1 on v0

v1 whole, which is shorter than its diff:
```python
import functools

import jax
import jax.numpy as jnp
from jax import lax
from jax.experimental import pallas as pl
from jax.experimental.pallas import tpu as pltpu
from jax.sharding import PartitionSpec as P

F32 = jnp.float32
BF16 = jnp.bfloat16
MESH = pl.DeviceIdType.MESH


def mixer_kernel(
    n,
    m,
    counts,
    partner,
    tokens,
    f1_hbm,
    f2,
    gain,
    bias,
    reading,
    gated,
    contrast,
    tok,
    f1,
    mixed,
    vals,
    inps,
    w,
    outs,
    part,
    pbuf,
    gbuf,
    local_sem,
    out_sem,
    isend,
    irecv,
    vsend,
    vrecv,
    psend,
    precv,
    gsend,
    grecv,
):
    docs, blk, chan = tokens.shape
    rows = blk // n
    me = lax.axis_index("seq")
    my_doc = lax.axis_index("doc")
    doc_start = my_doc * docs

    def peer(k):
        return lax.rem(me + k, n)

    def doc_peer(k):
        return lax.rem(my_doc + k, m)

    load_tok = pltpu.make_async_copy(tokens, tok, local_sem.at[0])
    load_f1 = pltpu.make_async_copy(f1_hbm.at[0], f1, local_sem.at[1])
    own_slice = pl.ds(pl.multiple_of(me * rows, rows), rows)
    own_in = pltpu.make_async_copy(
        tokens.at[:, own_slice], inps.at[:, own_slice], local_sem.at[2]
    )
    load_tok.start()
    load_f1.start()
    own_in.start()

    barrier = pltpu.get_barrier_semaphore()
    for k in range(1, n):
        pl.semaphore_signal(barrier, inc=1, device_id={"seq": peer(k)}, device_id_type=MESH)
    for k in range(1, m):
        pl.semaphore_signal(barrier, inc=1, device_id={"doc": doc_peer(k)}, device_id_type=MESH)
    pl.semaphore_wait(barrier, n - 1 + m - 1)

    order = sorted(range(1, n), key=lambda k: abs(k - n // 2))
    sends_in = []
    for k in order:
        theirs = pl.ds(pl.multiple_of(peer(k) * rows, rows), rows)
        copy = pltpu.make_async_remote_copy(
            src_ref=tokens.at[:, theirs],
            dst_ref=inps.at[:, own_slice],
            send_sem=isend.at[k],
            recv_sem=irecv.at[k],
            device_id={"seq": peer(k)},
            device_id_type=MESH,
        )
        copy.start()
        sends_in.append(copy)

    load_tok.wait()
    load_f1.wait()
    tile = 256
    sends_val = []
    for d in range(docs):
        keep = (counts[doc_start + d] > me).astype(F32)

        @pl.loop(0, blk // tile)
        def _(t):
            cols = pl.ds(pl.multiple_of(t * tile, tile), tile)
            acc = lax.dot_general(
                f1[:, cols],
                tok[d],
                (((0,), (0,)), ((), ())),
                preferred_element_type=F32,
            )
            mixed[d, cols, :] = (acc * keep).astype(BF16)

        for k in order:
            theirs = pl.ds(pl.multiple_of(peer(k) * rows, rows), rows)
            copy = pltpu.make_async_remote_copy(
                src_ref=mixed.at[d, theirs],
                dst_ref=vals.at[d, own_slice],
                send_sem=vsend.at[d, k],
                recv_sem=vrecv.at[d, k],
                device_id={"seq": peer(k)},
                device_id_type=MESH,
            )
            copy.start()
            sends_val.append(copy)
        vals[d, own_slice, :] = mixed[d, own_slice, :]

    eye = lax.broadcasted_iota(jnp.int32, (rows, rows), 0) == lax.broadcasted_iota(
        jnp.int32, (rows, rows), 1
    )
    for p in range(n):
        for q in range(n):
            line = f2[p, q : q + 1, :].astype(F32)
            w[q * rows : (q + 1) * rows, p * rows : (p + 1) * rows] = jnp.where(
                eye, line, 0.0
            ).astype(BF16)

    own_in.wait()
    for copy in sends_in:
        copy.wait_recv()

    writes = []
    for d in range(docs):
        for copy in sends_val[d * (n - 1) : (d + 1) * (n - 1)]:
            copy.wait_recv()
        count = counts[doc_start + d]
        part[d : d + 1, :] = jnp.zeros((1, chan), F32)

        @pl.loop(0, n // 2)
        def _(pair):
            two = pl.ds(pl.multiple_of(pair * 2 * rows, 2 * rows), 2 * rows)
            second = jnp.dot(w[two, :], vals[d], preferred_element_type=F32)
            for h in range(2):
                q = pair * 2 + h
                keep = (q < count).astype(F32)
                here = pl.ds(pl.multiple_of(q * rows, rows), rows)
                grid = inps[d, here, :].astype(F32) * keep
                gate = 1.0 / (1.0 + jnp.exp(-(gain[...] * grid + bias[...])))
                full = second[h * rows : (h + 1) * rows] * gate
                outs[d, here, :] = full.astype(BF16)
                part[d : d + 1, :] += jnp.sum(full, axis=0, keepdims=True) * keep

        write = pltpu.make_async_copy(outs.at[d], gated.at[d], out_sem.at[d])
        write.start()
        writes.append(write)

    small = []
    for k in range(1, n):
        copy = pltpu.make_async_remote_copy(
            src_ref=part,
            dst_ref=pbuf.at[me],
            send_sem=psend.at[k],
            recv_sem=precv.at[k],
            device_id={"seq": peer(k)},
            device_id_type=MESH,
        )
        copy.start()
        small.append(copy)
    pbuf[me] = part[...]
    for copy in small:
        copy.wait_recv()
    total = pbuf[0]
    for p in range(1, n):
        total = total + pbuf[p]
    mine = []
    for d in range(docs):
        size = jnp.full((1, chan), counts[doc_start + d], jnp.int32).astype(F32) * blk
        mine.append(total[d : d + 1] / jnp.sqrt(size))
    mine = jnp.concatenate(mine, axis=0)
    gbuf[my_doc] = mine
    for k in range(1, m):
        copy = pltpu.make_async_remote_copy(
            src_ref=gbuf.at[my_doc],
            dst_ref=gbuf.at[my_doc],
            send_sem=gsend.at[k],
            recv_sem=grecv.at[k],
            device_id={"doc": doc_peer(k)},
            device_id_type=MESH,
        )
        copy.start()
        small.append(copy)
    for copy in small[n - 1 :]:
        copy.wait_recv()
    others = []
    for d in range(docs):
        want = partner[doc_start + d]
        other = jnp.zeros((1, chan), F32)
        for e in range(m * docs):
            pick = (want == e).astype(F32)
            other = other + gbuf[e // docs, e % docs : e % docs + 1, :] * pick
        others.append(other)
    diff = mine - jnp.concatenate(others, axis=0)
    contrast[...] = jnp.dot(
        diff, reading[...], precision=lax.Precision.HIGHEST, preferred_element_type=F32
    )

    for copy in sends_in + sends_val + small:
        copy.wait_send()
    for write in writes:
        write.wait()


def fused(n, m, tokens, factor_one, factor_two, gate_gain, gate_bias, block_counts, partner, reading):
    docs, blk, chan = tokens.shape
    dirs = reading.shape[1]
    smem = pl.BlockSpec(memory_space=pltpu.SMEM)
    vmem = pl.BlockSpec(memory_space=pltpu.VMEM)
    hbm = pl.BlockSpec(memory_space=pl.ANY)
    dma = pltpu.SemaphoreType.DMA
    rows = blk // n
    gated, contrast = pl.pallas_call(
        functools.partial(mixer_kernel, n, m),
        out_shape=(
            jax.ShapeDtypeStruct((docs, blk, chan), BF16),
            jax.ShapeDtypeStruct((docs, dirs), F32),
        ),
        in_specs=[smem, smem, hbm, hbm, vmem, vmem, vmem, vmem],
        out_specs=(hbm, vmem),
        scratch_shapes=[
            pltpu.VMEM((docs, blk, chan), BF16),
            pltpu.VMEM((blk, blk), BF16),
            pltpu.VMEM((docs, blk, chan), BF16),
            pltpu.VMEM((docs, blk, chan), BF16),
            pltpu.VMEM((docs, blk, chan), BF16),
            pltpu.VMEM((blk, blk), BF16),
            pltpu.VMEM((docs, blk, chan), BF16),
            pltpu.VMEM((docs, chan), F32),
            pltpu.VMEM((n, docs, chan), F32),
            pltpu.VMEM((m, docs, chan), F32),
            dma((3,)),
            dma((docs,)),
            dma((n,)),
            dma((n,)),
            dma((docs, n)),
            dma((docs, n)),
            dma((n,)),
            dma((n,)),
            dma((m,)),
            dma((m,)),
        ],
        compiler_params=pltpu.CompilerParams(
            collective_id=0, has_side_effects=True, vmem_limit_bytes=56 << 20
        ),
        name="mixer",
    )(
        block_counts,
        partner,
        tokens,
        factor_one,
        jnp.transpose(factor_two, (1, 2, 0)),
        gate_gain[None, :],
        gate_bias[None, :],
        reading,
    )
    return gated.reshape(docs, n, rows, chan), contrast


def plain(tokens, factor_one, factor_two, gate_gain, gate_bias, block_counts, partner, reading):
    doc_dev, _, chan = tokens.shape
    blocks_dev, blk_size = (factor_one.shape[0], factor_one.shape[1])
    all_blocks = factor_two.shape[1]
    all_docs = block_counts.shape[0]
    doc_start = lax.axis_index("doc") * doc_dev
    block_start = lax.axis_index("seq") * blocks_dev
    local_counts = lax.dynamic_slice_in_dim(block_counts, doc_start, doc_dev)
    block_ids = block_start + jnp.arange(blocks_dev, dtype=jnp.int32)
    inside = (block_ids[None, :] < local_counts[:, None]).astype(BF16)
    grid = tokens.reshape(doc_dev, blocks_dev, blk_size, chan) * inside[:, :, None, None]
    mixed = jnp.einsum("dbic,bij->dbjc", grid, factor_one, preferred_element_type=F32).astype(BF16)
    values_t = lax.all_to_all(mixed, "seq", split_axis=2, concat_axis=1, tiled=True)
    inputs_t = lax.all_to_all(grid, "seq", split_axis=2, concat_axis=1, tiled=True)
    second = jnp.einsum("dpjc,jpq->dqjc", values_t, factor_two, preferred_element_type=F32)
    full = second * jax.nn.sigmoid(gate_gain * inputs_t.astype(F32) + gate_bias)
    keep = (jnp.arange(all_blocks, dtype=jnp.int32)[None, :] < local_counts[:, None]).astype(F32)
    partial_value = jnp.sum(full * keep[:, :, None, None], axis=(1, 2))
    scale = 1.0 / jnp.sqrt(local_counts.astype(F32) * blk_size)
    mine = lax.psum(partial_value, "seq") * scale[:, None]
    pooled_all = lax.all_gather(mine, "doc", axis=0, tiled=True)
    local_partner = lax.dynamic_slice_in_dim(partner, doc_start, doc_dev)
    picker = (local_partner[:, None] == jnp.arange(all_docs, dtype=jnp.int32)[None, :]).astype(F32)
    other = jnp.dot(picker, pooled_all, precision=lax.Precision.HIGHEST)
    contrast = jnp.dot(mine - other, reading, precision=lax.Precision.HIGHEST)
    return full.astype(BF16), contrast


def solution(mesh):
    n, m = mesh.shape["seq"], mesh.shape["doc"]

    def shards(*args):
        factor_one, factor_two = args[1], args[2]
        lanes = factor_two.shape[0] % 128 == 0
        if factor_one.shape[0] == 1 and factor_two.shape[1] == n and n % 2 == 0 and lanes:
            return fused(n, m, *args)
        return plain(*args)

    placed = (
        P("doc", "seq", None),
        P("seq", None, None),
        P("seq", None, None),
        P(),
        P(),
        P(),
        P(),
        P(),
    )
    return jax.shard_map(
        shards,
        mesh=mesh,
        in_specs=placed,
        out_specs=(P("doc", None, "seq", None), P("doc", None)),
        check_vma=False,
    )
```

time: 255 us -> 205 us (0.80)
  Pallas kernels: 0 us -> 199 us
  waiting for transfers between devices: 158 us -> 0 us
  blocking collectives: 24.8 us -> 0 us
  matrix products: 22.2 us -> 0 us
  other arithmetic: 18.3 us -> 0 us
  local copies, waits for them, and re-layouts: 17.8 us -> 5.24 us
  starting transfers between devices: 12 us -> 0 us
    pallas_call x0 -> x1, Pallas kernels: none -> 199 us  [fused(): pl.pallas_call(functools.partial(mixer_kernel, n, m), out_shape=(jax.Shap...]
    all_to_all x2 -> x0, waiting for transfers between devices: 158 us -> none  [the longest x1 84.6 us: shards(): lax.all_to_all(mixed, 'seq', split_axis=2, concat_axis=1, tiled=True)]
    dot_general x4 -> x0, matrix products: 22.2 us -> none  [the longest x1 14.7 us: shards(): jnp.einsum('dpjc,jpq->dqjc', values_t, factor_two, preferred_element_type...]
    psum x1 -> x0, blocking collectives: 19.6 us -> none  [shards(): mine = lax.psum(partial_value, 'seq') * scale_local[:, None]]
    mul x2 -> x0, other arithmetic: 12.9 us -> none  [shards(): tokens.reshape(doc_dev, blocks_dev, blk_size, chan)]
    all_to_all x2 -> x0, starting transfers between devices: 12 us -> none  [the longest x1 7.25 us: shards(): lax.all_to_all(grid, 'seq', split_axis=2, concat_axis=1, tiled=True)]
    convert_element_type x1 -> x0, local copies, waits for them, and re-layouts: 7.88 us -> none  [shards(): mixed = jnp.einsum('dbic,bij->dbjc', grid, factor_one, preferred_element_...]
    all_gather x1 -> x0, blocking collectives: 5.18 us -> none  [shards(): pooled_all = lax.all_gather(mine, 'doc', axis=0, tiled=True)]
  transfers between devices with their start and end apart: 2 -> 0, of which waited for: 2 -> 0; matrix products, arithmetic and copies ran while one was open for 11% -> 0% of each run, Pallas kernels for 0% -> 0%
where the time goes in v1:
time: 205 us
  Pallas kernels  199 us (97%)
  local copies, waits for them, and re-layouts  5.24 us (3%)
    pallas_call x1, Pallas kernels, fused(): pl.pallas_call(functools.partial(mixer_kernel, n, m), out_shape=(jax.Shap...  199 us
    unnamed x4, local copies, waits for them, and re-layouts  5.24 us

profile of v1, /device:TPU:0, one launch (start us, length us, event | category | flops | bytes accessed | tf_op | source)
XLA Modules:
  0.0 204.9 jit_solution(13032113172463536875)
XLA Ops:
  0.6 199.0 %mixer.1 = (bf16[4,1024,512]{2,1,0:T(8,128)(2,1)}, f32[4,256]{1,0:T(4,128)}) custom-call(s32[16]{0:T(128)} %counts.1, s32[16]{0:T(128)} %partner.1, bf16[4,1024,512]{2,1,0:T(8,128)(2,1)} %tokens.1, bf16[1,1024,1024]{2,1,0:T(8,128)(2,1)} %f1_hbm.1, bf16[8,8,128]{2,1,0:T(8,128)(2,1)} %bitcast.5, f32[1,512]{1,0:T(1,128)} %bitcast.6, f32[1,512]{1,0:T(1,128)} %bitcast.7, ...), custom_call_target="tpu_custom_call" | custom-call | tf_op jit(solution)/shard_map/mixer/pallas_call | solution.py:228
  199.6 0.0 copy-start
  199.6 4.6 %copy.12 = bf16[4,8,128,512]{3,2,1,0:T(8,128)(2,1)} copy(bf16[4,8,128,512]{3,2,1,0:T(8,128)(2,1)} %bitcast.4) | data formatting | bytes 8388608
  204.3 0.0 copy-done
  204.3 0.6 copy.13
Async XLA Ops:
  199.6 4.7 %copy-start = (f32[4,256]{1,0:T(4,128)S(1)}, f32[4,256]{1,0:T(4,128)}, u32[]{:S(2)}) copy-start(f32[4,256]{1,0:T(4,128)} %get-tuple-element.9) | copy-start | bytes 12292

commit v2 on v1

--- a/solution.py
+++ b/solution.py
@@ -16,27 +16,26 @@
     n,
     m,
     counts,
-    partner,
     tokens,
     f1_hbm,
-    f2,
-    gain,
-    bias,
-    reading,
+    f2_hbm,
+    gain_hbm,
+    bias_hbm,
     gated,
-    contrast,
+    gbuf,
     tok,
     f1,
     mixed,
     vals,
     inps,
     w,
-    outs,
     part,
     pbuf,
-    gbuf,
+    gates,
+    f2,
+    gain,
+    bias,
     local_sem,
-    out_sem,
     isend,
     irecv,
     vsend,
@@ -64,9 +63,12 @@
     own_in = pltpu.make_async_copy(
         tokens.at[:, own_slice], inps.at[:, own_slice], local_sem.at[2]
     )
-    load_tok.start()
-    load_f1.start()
-    own_in.start()
+    tables = [
+        pltpu.make_async_copy(src, dst, local_sem.at[3 + i])
+        for i, (src, dst) in enumerate(
+            ((f2_hbm, f2), (gain_hbm, gain), (bias_hbm, bias))
+        )
+    ]
 
     barrier = pltpu.get_barrier_semaphore()
     for k in range(1, n):
@@ -90,9 +92,17 @@
         copy.start()
         sends_in.append(copy)
 
+    load_tok.start()
+    load_f1.start()
+    own_in.start()
+    for load in tables:
+        load.start()
     load_tok.wait()
     load_f1.wait()
     tile = 256
+    half = chan // 2
+    pieces = [(d, 0, chan) for d in range(docs - 1)]
+    pieces += [(docs - 1, 0, half), (docs - 1, half, half)]
     sends_val = []
     for d in range(docs):
         keep = (counts[doc_start + d] > me).astype(F32)
@@ -108,20 +118,26 @@
             )
             mixed[d, cols, :] = (acc * keep).astype(BF16)
 
-        for k in order:
-            theirs = pl.ds(pl.multiple_of(peer(k) * rows, rows), rows)
-            copy = pltpu.make_async_remote_copy(
-                src_ref=mixed.at[d, theirs],
-                dst_ref=vals.at[d, own_slice],
-                send_sem=vsend.at[d, k],
-                recv_sem=vrecv.at[d, k],
-                device_id={"seq": peer(k)},
-                device_id_type=MESH,
-            )
-            copy.start()
-            sends_val.append(copy)
+        for i, (doc, start, width) in enumerate(pieces):
+            if doc != d:
+                continue
+            lanes = pl.ds(start, width)
+            for k in order:
+                theirs = pl.ds(pl.multiple_of(peer(k) * rows, rows), rows)
+                copy = pltpu.make_async_remote_copy(
+                    src_ref=mixed.at[d, theirs, lanes],
+                    dst_ref=vals.at[d, own_slice, lanes],
+                    send_sem=vsend.at[i, k],
+                    recv_sem=vrecv.at[i, k],
+                    device_id={"seq": peer(k)},
+                    device_id_type=MESH,
+                )
+                copy.start()
+                sends_val.append(copy)
         vals[d, own_slice, :] = mixed[d, own_slice, :]
 
+    for load in tables:
+        load.wait()
     eye = lax.broadcasted_iota(jnp.int32, (rows, rows), 0) == lax.broadcasted_iota(
         jnp.int32, (rows, rows), 1
     )
@@ -136,30 +152,31 @@
     for copy in sends_in:
         copy.wait_recv()
 
-    writes = []
-    for d in range(docs):
-        for copy in sends_val[d * (n - 1) : (d + 1) * (n - 1)]:
+    part[...] = jnp.zeros_like(part)
+    for i, (d, start, width) in enumerate(pieces):
+        count = counts[doc_start + d]
+        lanes = pl.ds(start, width)
+        if start == 0:
+
+            @pl.loop(0, n)
+            def _(q):
+                here = pl.ds(pl.multiple_of(q * rows, rows), rows)
+                grid = inps[d, here, :].astype(F32) * (q < count).astype(F32)
+                gates[here, :] = 1.0 / (1.0 + jnp.exp(-(gain[...] * grid + bias[...])))
+
+        for copy in sends_val[i * (n - 1) : (i + 1) * (n - 1)]:
             copy.wait_recv()
-        count = counts[doc_start + d]
-        part[d : d + 1, :] = jnp.zeros((1, chan), F32)
 
         @pl.loop(0, n // 2)
         def _(pair):
             two = pl.ds(pl.multiple_of(pair * 2 * rows, 2 * rows), 2 * rows)
-            second = jnp.dot(w[two, :], vals[d], preferred_element_type=F32)
+            second = jnp.dot(w[two, :], vals[d, :, lanes], preferred_element_type=F32)
+            full = second * gates[two, lanes]
+            gated[d, two, lanes] = full.astype(BF16)
             for h in range(2):
-                q = pair * 2 + h
-                keep = (q < count).astype(F32)
-                here = pl.ds(pl.multiple_of(q * rows, rows), rows)
-                grid = inps[d, here, :].astype(F32) * keep
-                gate = 1.0 / (1.0 + jnp.exp(-(gain[...] * grid + bias[...])))
-                full = second[h * rows : (h + 1) * rows] * gate
-                outs[d, here, :] = full.astype(BF16)
-                part[d : d + 1, :] += jnp.sum(full, axis=0, keepdims=True) * keep
-
-        write = pltpu.make_async_copy(outs.at[d], gated.at[d], out_sem.at[d])
-        write.start()
-        writes.append(write)
+                keep = (pair * 2 + h < count).astype(F32)
+                line = jnp.sum(full[h * rows : (h + 1) * rows], axis=0, keepdims=True)
+                part[d : d + 1, lanes] += line * keep
 
     small = []
     for k in range(1, n):
@@ -198,23 +215,31 @@
         small.append(copy)
     for copy in small[n - 1 :]:
         copy.wait_recv()
+    for copy in sends_in + sends_val + small:
+        copy.wait_send()
+
+
+def finish_kernel(partner, held, pooled, reading_hbm, gated, contrast, reading, sem):
+    m, docs, chan = pooled.shape
+    load = pltpu.make_async_copy(reading_hbm, reading, sem.at[0])
+    load.start()
+    write = pltpu.make_async_copy(held, gated, sem.at[1])
+    write.start()
+    my_doc = lax.axis_index("doc")
     others = []
     for d in range(docs):
-        want = partner[doc_start + d]
+        want = partner[my_doc * docs + d]
         other = jnp.zeros((1, chan), F32)
         for e in range(m * docs):
             pick = (want == e).astype(F32)
-            other = other + gbuf[e // docs, e % docs : e % docs + 1, :] * pick
+            other = other + pooled[e // docs, e % docs : e % docs + 1, :] * pick
         others.append(other)
-    diff = mine - jnp.concatenate(others, axis=0)
+    diff = pooled[my_doc] - jnp.concatenate(others, axis=0)
+    load.wait()
     contrast[...] = jnp.dot(
         diff, reading[...], precision=lax.Precision.HIGHEST, preferred_element_type=F32
     )
-
-    for copy in sends_in + sends_val + small:
-        copy.wait_send()
-    for write in writes:
-        write.wait()
+    write.wait()
 
 
 def fused(n, m, tokens, factor_one, factor_two, gate_gain, gate_bias, block_counts, partner, reading):
@@ -225,14 +250,14 @@
     hbm = pl.BlockSpec(memory_space=pl.ANY)
     dma = pltpu.SemaphoreType.DMA
     rows = blk // n
-    gated, contrast = pl.pallas_call(
+    gated, pooled = pl.pallas_call(
         functools.partial(mixer_kernel, n, m),
         out_shape=(
-            jax.ShapeDtypeStruct((docs, blk, chan), BF16),
-            jax.ShapeDtypeStruct((docs, dirs), F32),
+            pltpu.VMEM((docs, blk, chan), BF16),
+            pltpu.VMEM((m, docs, chan), F32),
         ),
-        in_specs=[smem, smem, hbm, hbm, vmem, vmem, vmem, vmem],
-        out_specs=(hbm, vmem),
+        in_specs=[smem, hbm, hbm, hbm, hbm, hbm],
+        out_specs=(vmem, vmem),
         scratch_shapes=[
             pltpu.VMEM((docs, blk, chan), BF16),
             pltpu.VMEM((blk, blk), BF16),
@@ -240,16 +265,17 @@
             pltpu.VMEM((docs, blk, chan), BF16),
             pltpu.VMEM((docs, blk, chan), BF16),
             pltpu.VMEM((blk, blk), BF16),
-            pltpu.VMEM((docs, blk, chan), BF16),
             pltpu.VMEM((docs, chan), F32),
             pltpu.VMEM((n, docs, chan), F32),
-            pltpu.VMEM((m, docs, chan), F32),
-            dma((3,)),
-            dma((docs,)),
+            pltpu.VMEM((blk, chan), F32),
+            pltpu.VMEM((n, n, rows), BF16),
+            pltpu.VMEM((1, chan), F32),
+            pltpu.VMEM((1, chan), F32),
+            dma((6,)),
             dma((n,)),
             dma((n,)),
-            dma((docs, n)),
-            dma((docs, n)),
+            dma((docs + 1, n)),
+            dma((docs + 1, n)),
             dma((n,)),
             dma((n,)),
             dma((m,)),
@@ -261,14 +287,24 @@
         name="mixer",
     )(
         block_counts,
-        partner,
         tokens,
         factor_one,
         jnp.transpose(factor_two, (1, 2, 0)),
         gate_gain[None, :],
         gate_bias[None, :],
-        reading,
-    )
+    )
+    gated, contrast = pl.pallas_call(
+        finish_kernel,
+        out_shape=(
+            jax.ShapeDtypeStruct((docs, blk, chan), BF16),
+            jax.ShapeDtypeStruct((docs, dirs), F32),
+        ),
+        in_specs=[smem, vmem, vmem, hbm],
+        out_specs=(hbm, vmem),
+        scratch_shapes=[pltpu.VMEM((chan, dirs), F32), dma((2,))],
+        compiler_params=pltpu.CompilerParams(vmem_limit_bytes=16 << 20),
+        name="finish",
+    )(partner, gated, pooled, reading)
     return gated.reshape(docs, n, rows, chan), contrast
 
 

time: 205 us -> 202 us (0.985)
  local copies, waits for them, and re-layouts: 5.24 us -> 0.01 us
    unnamed x4, local copies, waits for them, and re-layouts: 5.24 us -> 0.01 us
    pallas_call x1 -> x2, Pallas kernels: 199 us -> 201 us  [the longest x1 198 us: fused(): pl.pallas_call(functools.partial(mixer_kernel, n, m), out_shape=(pltpu.VM...]
where the time goes in v2:
time: 202 us
  Pallas kernels  201 us (100%)
    pallas_call x1, Pallas kernels, fused(): pl.pallas_call(functools.partial(mixer_kernel, n, m), out_shape=(pltpu.VM...  198 us

profile of v2, /device:TPU:0, one launch (start us, length us, event | category | flops | bytes accessed | tf_op | source)
XLA Modules:
  0.0 201.6 jit_solution(12307099724440604190)
XLA Ops:
  0.6 0.0 copy-start
  0.6 0.0 copy-start.1
  0.7 197.7 %mixer.1 = (bf16[4,1024,512]{2,1,0:T(8,128)(2,1)S(1)}, f32[4,4,512]{2,1,0:T(4,128)S(1)}) custom-call(s32[16]{0:T(128)} %counts.1, bf16[4,1024,512]{2,1,0:T(8,128)(2,1)} %tokens.1, bf16[1,1024,1024]{2,1,0:T(8,128)(2,1)} %f1_hbm.1, bf16[8,8,128]{2,1,0:T(8,128)(2,1)} %bitcast.4, f32[1,512]{1,0:T(1,128)} %bitcast.5, f32[1,512]{1,0:T(1,128)} %bitcast.6), custom_call_target="tpu_custom_call" | custom-call | tf_op jit(solution)/shard_map/mixer/pallas_call | solution.py:253
  198.4 0.0 copy-done
  198.4 0.0 copy-done.1
  198.4 3.2 %finish.1 = (bf16[4,1024,512]{2,1,0:T(8,128)(2,1)}, f32[4,256]{1,0:T(4,128)}) custom-call(s32[16]{0:T(128)S(1)} %copy-done.1, bf16[4,1024,512]{2,1,0:T(8,128)(2,1)S(1)} %get-tuple-element.6.held, f32[4,4,512]{2,1,0:T(4,128)S(1)} %get-tuple-element.7.pooled, f32[512,256]{1,0:T(8,128)S(1)} %copy-done), custom_call_target="tpu_custom_call" | custom-call | tf_op jit(solution)/shard_map/finish/pallas_call | solution.py:296
Async XLA Ops:
  0.6 197.7 %copy-start = (f32[512,256]{1,0:T(8,128)S(1)}, f32[512,256]{1,0:T(8,128)}, u32[]{:S(2)}) copy-start(f32[512,256]{1,0:T(8,128)} %reading_hbm.1) | copy-start | bytes 1572868
  0.6 197.7 %copy-start.1 = (s32[16]{0:T(128)S(1)}, s32[16]{0:T(128)}, u32[]{:S(2)}) copy-start(s32[16]{0:T(128)} %partner.1) | copy-start | bytes 196

commit v3 on v2

--- a/solution.py
+++ b/solution.py
@@ -32,6 +32,7 @@
     part,
     pbuf,
     gates,
+    scale,
     f2,
     gain,
     bias,
@@ -153,6 +154,9 @@
         copy.wait_recv()
 
     part[...] = jnp.zeros_like(part)
+    for d in range(docs):
+        size = jnp.full((1, chan), counts[doc_start + d], jnp.int32).astype(F32) * blk
+        scale[d : d + 1, :] = 1.0 / jnp.sqrt(size)
     for i, (d, start, width) in enumerate(pieces):
         count = counts[doc_start + d]
         lanes = pl.ds(start, width)
@@ -191,17 +195,14 @@
         copy.start()
         small.append(copy)
     pbuf[me] = part[...]
+    for copy in sends_in + sends_val:
+        copy.wait_send()
     for copy in small:
         copy.wait_recv()
     total = pbuf[0]
     for p in range(1, n):
         total = total + pbuf[p]
-    mine = []
-    for d in range(docs):
-        size = jnp.full((1, chan), counts[doc_start + d], jnp.int32).astype(F32) * blk
-        mine.append(total[d : d + 1] / jnp.sqrt(size))
-    mine = jnp.concatenate(mine, axis=0)
-    gbuf[my_doc] = mine
+    gbuf[my_doc] = total * scale[...]
     for k in range(1, m):
         copy = pltpu.make_async_remote_copy(
             src_ref=gbuf.at[my_doc],
@@ -215,17 +216,20 @@
         small.append(copy)
     for copy in small[n - 1 :]:
         copy.wait_recv()
-    for copy in sends_in + sends_val + small:
+    for copy in small:
         copy.wait_send()
 
 
-def finish_kernel(partner, held, pooled, reading_hbm, gated, contrast, reading, sem):
+def finish_kernel(held, pooled, partner_hbm, reading_hbm, gated, contrast, reading, partner, sem):
     m, docs, chan = pooled.shape
-    load = pltpu.make_async_copy(reading_hbm, reading, sem.at[0])
+    write = pltpu.make_async_copy(held, gated, sem.at[0])
+    write.start()
+    load_partner = pltpu.make_async_copy(partner_hbm, partner, sem.at[1])
+    load_partner.start()
+    load = pltpu.make_async_copy(reading_hbm, reading, sem.at[2])
     load.start()
-    write = pltpu.make_async_copy(held, gated, sem.at[1])
-    write.start()
     my_doc = lax.axis_index("doc")
+    load_partner.wait()
     others = []
     for d in range(docs):
         want = partner[my_doc * docs + d]
@@ -268,6 +272,7 @@
             pltpu.VMEM((docs, chan), F32),
             pltpu.VMEM((n, docs, chan), F32),
             pltpu.VMEM((blk, chan), F32),
+            pltpu.VMEM((docs, chan), F32),
             pltpu.VMEM((n, n, rows), BF16),
             pltpu.VMEM((1, chan), F32),
             pltpu.VMEM((1, chan), F32),
@@ -299,12 +304,16 @@
             jax.ShapeDtypeStruct((docs, blk, chan), BF16),
             jax.ShapeDtypeStruct((docs, dirs), F32),
         ),
-        in_specs=[smem, vmem, vmem, hbm],
+        in_specs=[vmem, vmem, hbm, hbm],
         out_specs=(hbm, vmem),
-        scratch_shapes=[pltpu.VMEM((chan, dirs), F32), dma((2,))],
+        scratch_shapes=[
+            pltpu.VMEM((chan, dirs), F32),
+            pltpu.SMEM(partner.shape, jnp.int32),
+            dma((3,)),
+        ],
         compiler_params=pltpu.CompilerParams(vmem_limit_bytes=16 << 20),
         name="finish",
-    )(partner, gated, pooled, reading)
+    )(gated, pooled, partner, reading)
     return gated.reshape(docs, n, rows, chan), contrast
 
 

time: 202 us -> 201 us (level)
  no operation moved by 1% of the time
where the time goes in v3:
time: 201 us
  Pallas kernels  200 us (100%)
    pallas_call x1, Pallas kernels, fused(): pl.pallas_call(functools.partial(mixer_kernel, n, m), out_shape=(pltpu.VM...  198 us

profile of v3, /device:TPU:0, one launch (start us, length us, event | category | flops | bytes accessed | tf_op | source)
XLA Modules:
  0.0 200.9 jit_solution(18332083802275435329)
XLA Ops:
  0.6 0.0 copy-start
  0.6 0.0 copy-start.1
  0.7 197.6 %mixer.1 = (bf16[4,1024,512]{2,1,0:T(8,128)(2,1)S(1)}, f32[4,4,512]{2,1,0:T(4,128)S(1)}) custom-call(s32[16]{0:T(128)} %counts.1, bf16[4,1024,512]{2,1,0:T(8,128)(2,1)} %tokens.1, bf16[1,1024,1024]{2,1,0:T(8,128)(2,1)} %f1_hbm.1, bf16[8,8,128]{2,1,0:T(8,128)(2,1)} %bitcast.4, f32[1,512]{1,0:T(1,128)} %bitcast.5, f32[1,512]{1,0:T(1,128)} %bitcast.6), custom_call_target="tpu_custom_call" | custom-call | tf_op jit(solution)/shard_map/mixer/pallas_call | solution.py:257
  198.3 0.0 copy-done
  198.3 0.0 copy-done.1
  198.3 2.6 %finish.1 = (bf16[4,1024,512]{2,1,0:T(8,128)(2,1)}, f32[4,256]{1,0:T(4,128)}) custom-call(bf16[4,1024,512]{2,1,0:T(8,128)(2,1)S(1)} %get-tuple-element.6.held, f32[4,4,512]{2,1,0:T(4,128)S(1)} %get-tuple-element.7.pooled, s32[16]{0:T(128)S(1)} %copy-done.1, f32[512,256]{1,0:T(8,128)S(1)} %copy-done), custom_call_target="tpu_custom_call" | custom-call | tf_op jit(solution)/shard_map/finish/pallas_call | solution.py:301
Async XLA Ops:
  0.6 197.7 %copy-start = (f32[512,256]{1,0:T(8,128)S(1)}, f32[512,256]{1,0:T(8,128)}, u32[]{:S(2)}) copy-start(f32[512,256]{1,0:T(8,128)} %reading_hbm.1) | copy-start | bytes 1572868
  0.6 197.7 %copy-start.1 = (s32[16]{0:T(128)S(1)}, s32[16]{0:T(128)}, u32[]{:S(2)}) copy-start(s32[16]{0:T(128)} %partner_hbm.1) | copy-start | bytes 196
